TPU v7x, 128 devices: a whole 4x4x4 slice. The times are simulated.
128 devices in a mesh: row: 8 (over x, z_hi), col: 16 (over y, z_lo, core).
Axes of the slice: x: 4, y: 4, z: 4 (z_hi: 2, z_lo: 2; z = z_hi * 2 + z_lo), core: 2. Of those that a mesh axis runs over, the one named last changes fastest.
Arguments:
- matrix: float32 [16384, 16384], P('row', 'col'), may hold values from -6 to 6
- factor_inverse: float32 [512, 512], replicated, may hold values from -0.25 to 0.25
- panel: int32 [1], replicated, may hold values from 0 to 31
- split_index: int32 [1], replicated, may hold values from 4096 to 12288
Outputs:
- halves: float32 [16384, 512], P('col')
All inputs are finite; a program needn't handle non-finite values.
Results may differ from a plain program's by a relative error of at most 0.000071.
Values sent between devices are 32-bit elements; how exact they have to be, the bound alone decides.
No kernel may reach another device: no remote copies, remote signals or barrier semaphores. Data moves between devices by JAX's collectives and lax.ppermute only.
A program may use at most 64 MiB of HBM per device.

v0:
```python
import jax
import jax.numpy as jnp
from jax import lax
from jax.sharding import PartitionSpec as P


def broadcast(x, axis, root):
    mine = lax.axis_index(axis) == root
    return lax.psum(jnp.where(mine, x, jnp.zeros_like(x)), axis)


def identity_rows(first, count, start, width):
    rows_global = first + jnp.arange(count, dtype=jnp.int32)
    return (rows_global[:, None] == start + jnp.arange(width, dtype=jnp.int32)[None, :]).astype(
        jnp.float32
    )


def per_device(matrix, factor_inverse, panel, split_index):
    rows_loc, cols_loc = matrix.shape
    width = factor_inverse.shape[0]
    ncol = lax.axis_size("col")
    nrow = lax.axis_size("row")
    order = cols_loc * ncol
    col_idx = lax.axis_index("col")
    row_idx = lax.axis_index("row")
    start = panel[0] * width
    owner = start // cols_loc
    offset = start - owner * cols_loc
    piece = lax.dynamic_slice_in_dim(matrix, offset, width, 1)
    columns = broadcast(piece, "col", owner)
    partial_value = lax.dot_general(
        matrix,
        columns,
        (((0,), (0,)), ((), ())),
        precision=lax.Precision.HIGHEST,
        preferred_element_type=jnp.float32,
    )
    gram = lax.psum(partial_value, "row") / order + identity_rows(
        col_idx * cols_loc, cols_loc, start, width
    )
    factor = lax.dot_general(
        gram,
        factor_inverse,
        (((1,), (1,)), ((), ())),
        precision=lax.Precision.HIGHEST,
        preferred_element_type=jnp.float32,
    )
    per_dev = rows_loc // ncol
    ratio = ncol // nrow
    col_rows = order // ncol
    mine = identity_rows(row_idx * rows_loc + col_idx * per_dev, per_dev, start, width)
    product = lax.psum_scatter(
        jnp.dot(
            matrix, factor, precision=lax.Precision.HIGHEST, preferred_element_type=jnp.float32
        ),
        "col",
        scatter_dimension=0,
        tiled=True,
    )
    projector = 0.5 * (mine + product)
    row_stack = lax.all_gather(projector, "col", axis=0, tiled=True)
    selected = lax.dynamic_slice_in_dim(row_stack, col_idx % ratio * col_rows, col_rows, 0)
    gathered = broadcast(selected, "row", col_idx // ratio)
    rows_global = col_idx * col_rows + jnp.arange(col_rows, dtype=jnp.int32)
    keep = (rows_global < order // 2) == (rows_global < split_index[0])
    return jnp.where(keep[:, None], gathered, jnp.float32(0.0))


def solution(mesh):
    placed = (P("row", "col"), P(), P(), P())
    return jax.shard_map(
        per_device, mesh=mesh, in_specs=placed, out_specs=P("col", None), check_vma=False
    )
```

profile of v0, /device:TPU:0, one launch (start us, length us, event | category | flops | bytes accessed | tf_op | source)
XLA Modules:
  0.0 554.6 jit_solution(17478450682226694974)
XLA Ops:
  6.5 0.0 copy-start
  6.5 0.0 all-reduce.4.cloned.1.call-start
  7.3 4.7 dynamic-slice_select_fusion
  12.0 0.0 all-reduce.4.cloned.1.call-update
  12.0 0.0 all-reduce.6.cloned.1.call-start
  12.0 133.4 %all-reduce.4.cloned.1.call-done = f32[2048,512]{1,0:T(8,128)} async-done(((f32[2048,512]{1,0:T(8,128)}), f32[2048,512]{1,0:T(8,128)}) %all-reduce.4.cloned.1.call-update) | async-done | bytes 4194320 | tf_op jit(solution)/shard_map/psum | solution.py:9
  145.5 18.0 %convolution_bitcast_fusion.1 = f32[1024,512]{0,1:T(8,128)} fusion(f32[2048,512]{1,0:T(8,128)} %all-reduce.4.cloned.1.call-done, f32[2048,1024]{1,0:T(8,128)} %param.4), kind=kOutput, calls=%fused_computation.8 | convolution fusion | flops 12884901888 | bytes 14680064 | tf_op jit(solution)/shard_map/dot_general | solution.py:32
  163.5 0.0 all-reduce.6.cloned.1.call-update
  163.5 0.2 reduce-scatter.2.cloned.1.call-start
  163.7 112.2 %all-reduce.6.cloned.1.call-done = f32[1024,512]{0,1:T(8,128)} async-done(((f32[1024,512]{0,1:T(8,128)}), f32[1024,512]{0,1:T(8,128)}) %all-reduce.6.cloned.1.call-update) | async-done | bytes 2097168 | tf_op jit(solution)/shard_map/psum | solution.py:39
  276.0 8.4 %fusion = f32[1024,512]{1,0:T(8,128)S(1)} fusion(f32[512,512]{1,0:T(8,128)S(1)} %copy-done, f32[1024,512]{0,1:T(8,128)} %all-reduce.6.cloned.1.call-done, s32[1024]{0:T(1024)S(1)} %iota_add_fusion, s32[512]{0:T(512)S(1)} %iota_add_fusion.1), kind=kOutput, calls=%fused_computation.3 | convolution fusion | flops 3223322624 | bytes 5249024 | tf_op jit(solution)/shard_map/dot_general | solution.py:42
  284.4 31.0 %convolution_bitcast_fusion = f32[2048,512]{0,1:T(8,128)} fusion(f32[1024,512]{1,0:T(8,128)S(1)} %fusion, f32[2048,1024]{1,0:T(8,128)} %param.4), kind=kOutput, calls=%fused_computation.1 | convolution fusion | flops 12884901888 | bytes 14680064 | tf_op jit(solution)/shard_map/dot_general | solution.py:54
  315.4 0.0 reduce-scatter.2.cloned.1.call-update
  315.4 0.0 all-gather.2.cloned.1.call-start
  315.5 67.4 %reduce-scatter.2.cloned.1.call-done = f32[128,512]{0,1:T(8,128)} async-done(((f32[2048,512]{0,1:T(8,128)}), f32[128,512]{0,1:T(8,128)}) %reduce-scatter.2.cloned.1.call-update) | async-done | bytes 262160 | tf_op jit(solution)/shard_map/reduce_scatter | solution.py:53
  382.9 1.8 add_multiply_fusion
  384.6 0.0 all-gather.2.cloned.1.call-update
  384.7 0.0 all-reduce.8.cloned.1.call-start
  384.8 43.7 %all-gather.2.cloned.1.call-done = f32[2048,512]{0,1:T(8,128)} async-done(((f32[128,512]{0,1:T(8,128)}), f32[2048,512]{0,1:T(8,128)}) %all-gather.2.cloned.1.call-update) | async-done | bytes 4194320 | tf_op jit(solution)/shard_map/all_gather | solution.py:62
  428.5 3.2 dynamic-slice_select_fusion.1
  431.7 0.0 all-reduce.8.cloned.1.call-update
  432.4 112.1 %all-reduce.8.cloned.1.call-done = f32[1024,512]{0,1:T(8,128)} async-done(((f32[1024,512]{0,1:T(8,128)}), f32[1024,512]{0,1:T(8,128)}) %all-reduce.8.cloned.1.call-update) | async-done | bytes 2097168 | tf_op jit(solution)/shard_map/psum | solution.py:9
  544.5 1.8 broadcast_select_fusion
  546.3 1.8 copy.5
  (5 shorter events, 0.0 us)
Async XLA Ops:
  6.5 269.4 %copy-start = (f32[512,512]{1,0:T(8,128)S(1)}, f32[512,512]{1,0:T(8,128)}, u32[]{:S(2)}) copy-start(f32[512,512]{1,0:T(8,128)} %param.5) | copy-start | bytes 3145732
  6.5 138.9 %all-reduce.4.cloned.1.call-start = ((), (), s32[]{:S(2)}) async-start(), calls=%async_computation.1 | async-start | bytes 8388608 | tf_op jit(solution)/shard_map/psum | solution.py:9
  12.0 264.0 %all-reduce.6.cloned.1.call-start = ((), (), s32[]{:S(2)}) async-start(), calls=%async_computation.2 | async-start | bytes 4194304 | tf_op jit(solution)/shard_map/psum | solution.py:39
  163.5 219.4 %reduce-scatter.2.cloned.1.call-start = ((), (), s32[]{:S(2)}) async-start(), calls=%async_computation.3 | async-start | bytes 4456448 | tf_op jit(solution)/shard_map/reduce_scatter | solution.py:53
  315.4 113.1 %all-gather.2.cloned.1.call-start = ((), (), s32[]{:S(2)}) async-start(), calls=%async_computation.4 | async-start | bytes 4456448 | tf_op jit(solution)/shard_map/all_gather | solution.py:62
  384.7 159.8 %all-reduce.8.cloned.1.call-start = ((), (), s32[]{:S(2)}) async-start(), calls=%async_computation.5 | async-start | bytes 4194304 | tf_op jit(solution)/shard_map/psum | solution.py:9
Sparse Core Ops, SparseCore 0:
  12.1 133.3 all-reduce.3
  163.6 112.3 all-reduce.5
  315.5 67.3 reduce-scatter.1
  384.8 43.6 all-gather.1
  431.8 112.6 all-reduce.7
where the time goes:
time: 555 us
  waiting for transfers between devices  469 us (85%)
  matrix products  57.4 us (10%)
  between operations  14.6 us (3%)
  other arithmetic  11.4 us (2%)
    psum x2, waiting for transfers between devices, broadcast(): return lax.psum(jnp.where(mine, x, jnp.zeros_like(x)), axis)  246 us
    psum x1, waiting for transfers between devices, per_device(): lax.psum(partial_value, 'row') / order  112 us
    reduce_scatter x1, waiting for transfers between devices, per_device(): lax.psum_scatter(jnp.dot(matrix, factor, precision=lax.Precision.HIGHEST,...  67.4 us
    all_gather x1, waiting for transfers between devices, per_device(): row_stack = lax.all_gather(projector, 'col', axis=0, tiled=True)  43.7 us
    dot_general x1, matrix products, per_device(): jnp.dot(matrix, factor, precision=lax.Precision.HIGHEST, preferred_elemen...  31 us
    dot_general x1, matrix products, per_device(): lax.dot_general(matrix, columns, (((0,), (0,)), ((), ())), precision=lax....  18 us
  transfers between devices with their start and end apart: 5, of which 5 were waited for; matrix products, arithmetic and copies ran while one was open for 0% of the time, Pallas kernels for 0%

commit v1 on v0

--- a/solution.py
+++ b/solution.py
@@ -1,7 +1,16 @@
+import functools
 import jax
 import jax.numpy as jnp
 from jax import lax
 from jax.sharding import PartitionSpec as P
+from jax.lax import all_gather
+
+
+def finish_body(arr, shard_axis):
+    return jnp.sum(all_gather(arr, axis_name=shard_axis), axis=0)
+
+
+advance_the_plate = functools.partial(finish_body, shard_axis="row")
 
 
 def broadcast(x, axis, root):
@@ -36,7 +45,7 @@
         precision=lax.Precision.HIGHEST,
         preferred_element_type=jnp.float32,
     )
-    gram = lax.psum(partial_value, "row") / order + identity_rows(
+    gram = advance_the_plate(partial_value) / order + identity_rows(
         col_idx * cols_loc, cols_loc, start, width
     )
     factor = lax.dot_general(

time: 555 us -> 651 us (1.17)
  waiting for transfers between devices: 469 us -> 541 us
  local copies, waits for them, and re-layouts: 1.82 us -> 21.5 us
    all_gather x0 -> x1, waiting for transfers between devices: none -> 186 us  [finish_body(): return jnp.sum(all_gather(arr, axis_name=shard_axis), axis=0)]
    psum x1 -> x0, waiting for transfers between devices: 112 us -> none  [per_device(): lax.psum(partial_value, 'row') / order]
    unnamed x2 -> x3, local copies, waits for them, and re-layouts: 0.01 us -> 19.7 us
where the time goes in v1:
time: 651 us; the launch traced here: 650 us
  waiting for transfers between devices  541 us (83%)
  matrix products  55.8 us (9%)
  local copies, waits for them, and re-layouts  21.5 us (3%)
  other arithmetic  17 us (3%)
  between operations  14.7 us (2%)
    psum x2, waiting for transfers between devices, broadcast(): return lax.psum(jnp.where(mine, x, jnp.zeros_like(x)), axis)  246 us
    all_gather x1, waiting for transfers between devices, finish_body(): return jnp.sum(all_gather(arr, axis_name=shard_axis), axis=0)  186 us
    reduce_scatter x1, waiting for transfers between devices, per_device(): lax.psum_scatter(jnp.dot(matrix, factor, precision=lax.Precision.HIGHEST,...  66 us
    all_gather x1, waiting for transfers between devices, per_device(): row_stack = lax.all_gather(projector, 'col', axis=0, tiled=True)  43.8 us
    dot_general x1, matrix products, per_device(): jnp.dot(matrix, factor, precision=lax.Precision.HIGHEST, preferred_elemen...  31 us
    unnamed x3, local copies, waits for them, and re-layouts  19.7 us
    dot_general x1, matrix products, per_device(): lax.dot_general(matrix, columns, (((0,), (0,)), ((), ())), precision=lax....  18 us
  transfers between devices with their start and end apart: 5, of which 5 were waited for; matrix products, arithmetic and copies ran while one was open for 0% of the time, Pallas kernels for 0%

profile of v1, /device:TPU:0, one launch (start us, length us, event | category | flops | bytes accessed | tf_op | source)
XLA Modules:
  0.0 650.4 jit_solution(16842085734590490022)
XLA Ops:
  7.3 4.7 dynamic-slice_select_fusion
  12.0 0.0 all-reduce.3.cloned.1.call-update
  12.0 0.0 all-gather.6.cloned.1.call-start
  12.0 133.4 %all-reduce.3.cloned.1.call-done = f32[2048,512]{1,0:T(8,128)} async-done(((f32[2048,512]{1,0:T(8,128)}), f32[2048,512]{1,0:T(8,128)}) %all-reduce.3.cloned.1.call-update) | async-done | bytes 4194320 | tf_op jit(solution)/shard_map/psum | solution.py:18
  145.5 18.0 %convolution_bitcast_fusion.1 = f32[1024,512]{0,1:T(8,128)} fusion(f32[2048,512]{1,0:T(8,128)} %all-reduce.3.cloned.1.call-done, f32[2048,1024]{1,0:T(8,128)} %param.4), kind=kOutput, calls=%fused_computation.9 | convolution fusion | flops 12884901888 | bytes 14680064 | tf_op jit(solution)/shard_map/dot_general | solution.py:41
  163.5 0.0 all-gather.6.cloned.1.call-update
  163.5 0.2 reduce-scatter.2.cloned.1.call-start
  163.7 185.7 %all-gather.6.cloned.1.call-done = f32[8192,512]{0,1:T(8,128)} async-done(((f32[1024,512]{0,1:T(8,128)}), f32[8192,512]{0,1:T(8,128)}) %all-gather.6.cloned.1.call-update) | async-done | bytes 16777232 | tf_op jit(solution)/shard_map/all_gather | solution.py:10
  349.4 19.7 %copy.7 = f32[64,8,8,1024]{3,2,1,0:T(8,128)S(1)} copy(f32[64,8,8,1024]{3,1,2,0:T(8,128)} %bitcast.17) | data formatting | bytes 33554432
  369.1 5.6 bitcast_reduce_fusion
  374.7 6.8 %fusion = f32[1024,512]{1,0:T(8,128)S(1)} fusion(f32[512,512]{1,0:T(8,128)S(1)} %copy-done, f32[1024,512]{0,1:T(8,128)S(1)} %bitcast_reduce_fusion, s32[1024]{0:T(1024)S(1)} %iota_add_fusion, s32[512]{0:T(512)S(1)} %iota_add_fusion.1), kind=kOutput, calls=%fused_computation.4 | convolution fusion | flops 3223322624 | bytes 5249024 | tf_op jit(solution)/shard_map/dot_general | solution.py:51
  381.5 31.0 %convolution_bitcast_fusion = f32[2048,512]{0,1:T(8,128)} fusion(f32[1024,512]{1,0:T(8,128)S(1)} %fusion, f32[2048,1024]{1,0:T(8,128)} %param.4), kind=kOutput, calls=%fused_computation.2 | convolution fusion | flops 12884901888 | bytes 14680064 | tf_op jit(solution)/shard_map/dot_general | solution.py:63
  412.6 0.0 reduce-scatter.2.cloned.1.call-update
  412.6 0.0 all-gather.4.cloned.1.call-start
  412.7 66.0 %reduce-scatter.2.cloned.1.call-done = f32[128,512]{0,1:T(8,128)} async-done(((f32[2048,512]{0,1:T(8,128)}), f32[128,512]{0,1:T(8,128)}) %reduce-scatter.2.cloned.1.call-update) | async-done | bytes 262160 | tf_op jit(solution)/shard_map/reduce_scatter | solution.py:62
  478.6 1.8 add_multiply_fusion
  480.4 0.0 all-gather.4.cloned.1.call-update
  480.4 0.0 all-reduce.5.cloned.1.call-start
  480.5 43.8 %all-gather.4.cloned.1.call-done = f32[2048,512]{0,1:T(8,128)} async-done(((f32[128,512]{0,1:T(8,128)}), f32[2048,512]{0,1:T(8,128)}) %all-gather.4.cloned.1.call-update) | async-done | bytes 4194320 | tf_op jit(solution)/shard_map/all_gather | solution.py:71
  524.3 3.2 dynamic-slice_select_fusion.1
  527.5 0.0 all-reduce.5.cloned.1.call-update
  528.2 112.1 %all-reduce.5.cloned.1.call-done = f32[1024,512]{0,1:T(8,128)} async-done(((f32[1024,512]{0,1:T(8,128)}), f32[1024,512]{0,1:T(8,128)}) %all-reduce.5.cloned.1.call-update) | async-done | bytes 2097168 | tf_op jit(solution)/shard_map/psum | solution.py:18
  640.3 1.8 broadcast_select_fusion
  642.1 1.8 copy.6
  (7 shorter events, 0.0 us)
Async XLA Ops:
  6.5 368.2 %copy-start = (f32[512,512]{1,0:T(8,128)S(1)}, f32[512,512]{1,0:T(8,128)}, u32[]{:S(2)}) copy-start(f32[512,512]{1,0:T(8,128)} %param.5) | copy-start | bytes 3145732
  6.5 138.9 %all-reduce.3.cloned.1.call-start = ((), (), s32[]{:S(2)}) async-start(), calls=%async_computation.1 | async-start | bytes 8388608 | tf_op jit(solution)/shard_map/psum | solution.py:18
  12.0 337.4 %all-gather.6.cloned.1.call-start = ((), (), s32[]{:S(2)}) async-start(), calls=%async_computation.5 | async-start | bytes 18874368 | tf_op jit(solution)/shard_map/all_gather | solution.py:10
  163.5 315.1 %reduce-scatter.2.cloned.1.call-start = ((), (), s32[]{:S(2)}) async-start(), calls=%async_computation.2 | async-start | bytes 4456448 | tf_op jit(solution)/shard_map/reduce_scatter | solution.py:62
  412.6 111.7 %all-gather.4.cloned.1.call-start = ((), (), s32[]{:S(2)}) async-start(), calls=%async_computation.3 | async-start | bytes 4456448 | tf_op jit(solution)/shard_map/all_gather | solution.py:71
  480.4 159.9 %all-reduce.5.cloned.1.call-start = ((), (), s32[]{:S(2)}) async-start(), calls=%async_computation.4 | async-start | bytes 4194304 | tf_op jit(solution)/shard_map/psum | solution.py:18
Sparse Core Ops, SparseCore 0:
  12.1 133.3 all-reduce.2
  163.6 185.7 all-gather.5
  412.7 65.8 reduce-scatter.1
  480.6 43.6 all-gather.3
  527.6 112.6 all-reduce.4

commit v2 on v0

--- a/solution.py
+++ b/solution.py
@@ -59,7 +59,8 @@
         tiled=True,
     )
     projector = 0.5 * (mine + product)
-    row_stack = lax.all_gather(projector, "col", axis=0, tiled=True)
+    sent = jnp.stack([projector] * lax.axis_size("col"))
+    row_stack = jnp.concatenate(lax.all_to_all(sent, "col", 0, 0), axis=0)
     selected = lax.dynamic_slice_in_dim(row_stack, col_idx % ratio * col_rows, col_rows, 0)
     gathered = broadcast(selected, "row", col_idx // ratio)
     rows_global = col_idx * col_rows + jnp.arange(col_rows, dtype=jnp.int32)

time: 555 us -> 576 us (1.038)
  waiting for transfers between devices: 469 us -> 484 us
    all_to_all x0 -> x1, waiting for transfers between devices: none -> 52 us  [per_device(): row_stack = jnp.concatenate(lax.all_to_all(sent, 'col', 0, 0), axis=0)]
    all_gather x1 -> x0, waiting for transfers between devices: 43.7 us -> none  [per_device(): row_stack = lax.all_gather(projector, 'col', axis=0, tiled=True)]
    psum x2, waiting for transfers between devices: 246 us -> 252 us  [broadcast(): return lax.psum(jnp.where(mine, x, jnp.zeros_like(x)), axis)]
where the time goes in v2:
time: 576 us; the launch traced here: 575 us
  waiting for transfers between devices  484 us (84%)
  matrix products  57.3 us (10%)
  between operations  14.7 us (3%)
  other arithmetic  12 us (2%)
    psum x2, waiting for transfers between devices, broadcast(): return lax.psum(jnp.where(mine, x, jnp.zeros_like(x)), axis)  252 us
    psum x1, waiting for transfers between devices, per_device(): lax.psum(partial_value, 'row') / order  113 us
    reduce_scatter x1, waiting for transfers between devices, per_device(): lax.psum_scatter(jnp.dot(matrix, factor, precision=lax.Precision.HIGHEST,...  67.4 us
    all_to_all x1, waiting for transfers between devices, per_device(): row_stack = jnp.concatenate(lax.all_to_all(sent, 'col', 0, 0), axis=0)  52 us
    dot_general x1, matrix products, per_device(): jnp.dot(matrix, factor, precision=lax.Precision.HIGHEST, preferred_elemen...  30.9 us
    dot_general x1, matrix products, per_device(): lax.dot_general(matrix, columns, (((0,), (0,)), ((), ())), precision=lax....  18 us
  transfers between devices with their start and end apart: 5, of which 5 were waited for; matrix products, arithmetic and copies ran while one was open for 0% of the time, Pallas kernels for 0%

profile of v2, /device:TPU:0, one launch (start us, length us, event | category | flops | bytes accessed | tf_op | source)
XLA Modules:
  0.0 575.4 jit_solution(2759552142055198964)
XLA Ops:
  6.5 0.0 copy-start
  6.5 0.0 all-reduce.4.cloned.1.call-start
  7.3 4.7 dynamic-slice_select_fusion
  12.0 0.0 all-reduce.4.cloned.1.call-update
  12.0 0.0 all-reduce.6.cloned.1.call-start
  12.0 133.4 %all-reduce.4.cloned.1.call-done = f32[2048,512]{1,0:T(8,128)} async-done(((f32[2048,512]{1,0:T(8,128)}), f32[2048,512]{1,0:T(8,128)}) %all-reduce.4.cloned.1.call-update) | async-done | bytes 4194320 | tf_op jit(solution)/shard_map/psum | solution.py:9
  145.5 18.0 %convolution_bitcast_fusion.1 = f32[1024,512]{0,1:T(8,128)} fusion(f32[2048,512]{1,0:T(8,128)} %all-reduce.4.cloned.1.call-done, f32[2048,1024]{1,0:T(8,128)} %param.4), kind=kOutput, calls=%fused_computation.8 | convolution fusion | flops 12884901888 | bytes 14680064 | tf_op jit(solution)/shard_map/dot_general | solution.py:32
  163.5 0.0 all-reduce.6.cloned.1.call-update
  163.5 0.2 reduce-scatter.2.cloned.1.call-start
  163.7 112.5 %all-reduce.6.cloned.1.call-done = f32[1024,512]{0,1:T(8,128)} async-done(((f32[1024,512]{0,1:T(8,128)}), f32[1024,512]{0,1:T(8,128)}) %all-reduce.6.cloned.1.call-update) | async-done | bytes 2097168 | tf_op jit(solution)/shard_map/psum | solution.py:39
  276.3 8.4 %fusion = f32[1024,512]{1,0:T(8,128)S(1)} fusion(f32[512,512]{1,0:T(8,128)S(1)} %copy-done, f32[1024,512]{0,1:T(8,128)} %all-reduce.6.cloned.1.call-done, s32[1024]{0:T(1024)S(1)} %iota_add_fusion, s32[512]{0:T(512)S(1)} %iota_add_fusion.1), kind=kOutput, calls=%fused_computation.3 | convolution fusion | flops 3223322624 | bytes 5249024 | tf_op jit(solution)/shard_map/dot_general | solution.py:42
  284.7 30.9 %convolution_bitcast_fusion = f32[2048,512]{0,1:T(8,128)} fusion(f32[1024,512]{1,0:T(8,128)S(1)} %fusion, f32[2048,1024]{1,0:T(8,128)} %param.4), kind=kOutput, calls=%fused_computation.1 | convolution fusion | flops 12884901888 | bytes 14680064 | tf_op jit(solution)/shard_map/dot_general | solution.py:54
  315.6 0.0 reduce-scatter.2.cloned.1.call-update
  315.7 67.4 %reduce-scatter.2.cloned.1.call-done = f32[128,512]{0,1:T(8,128)} async-done(((f32[2048,512]{0,1:T(8,128)}), f32[128,512]{0,1:T(8,128)}) %reduce-scatter.2.cloned.1.call-update) | async-done | bytes 262160 | tf_op jit(solution)/shard_map/reduce_scatter | solution.py:53
  383.1 1.1 add_multiply_fusion
  384.1 0.1 copy.5
  384.3 2.5 stack.2
  386.8 4.5 all-to-all-start
  391.3 0.0 all-reduce.8.cloned.1.call-start
  391.4 52.0 %all-to-all-done = f32[16,128,512]{2,1,0:T(8,128)} async-done(((f32[16,128,512]{2,1,0:T(8,128)}), f32[16,128,512]{2,1,0:T(8,128)}, u32[]{:S(2)}, u32[]{:S(2)}) %all-to-all-start) | async-done | bytes 4194336 | tf_op jit(solution)/shard_map/all_to_all | solution.py:63
  443.5 3.1 dynamic-slice_select_fusion.1
  446.6 0.0 all-reduce.8.cloned.1.call-update
  447.3 118.5 %all-reduce.8.cloned.1.call-done = f32[1024,512]{1,0:T(8,128)} async-done(((f32[1024,512]{1,0:T(8,128)}), f32[1024,512]{1,0:T(8,128)}) %all-reduce.8.cloned.1.call-update) | async-done | bytes 2097168 | tf_op jit(solution)/shard_map/psum | solution.py:9
  565.8 3.1 broadcast_select_fusion
  (5 shorter events, 0.0 us)
Async XLA Ops:
  6.5 269.7 %copy-start = (f32[512,512]{1,0:T(8,128)S(1)}, f32[512,512]{1,0:T(8,128)}, u32[]{:S(2)}) copy-start(f32[512,512]{1,0:T(8,128)} %param.5) | copy-start | bytes 3145732
  6.5 138.9 %all-reduce.4.cloned.1.call-start = ((), (), s32[]{:S(2)}) async-start(), calls=%async_computation.2 | async-start | bytes 8388608 | tf_op jit(solution)/shard_map/psum | solution.py:9
  12.0 264.3 %all-reduce.6.cloned.1.call-start = ((), (), s32[]{:S(2)}) async-start(), calls=%async_computation.3 | async-start | bytes 4194304 | tf_op jit(solution)/shard_map/psum | solution.py:39
  163.5 219.6 %reduce-scatter.2.cloned.1.call-start = ((), (), s32[]{:S(2)}) async-start(), calls=%async_computation.4 | async-start | bytes 4456448 | tf_op jit(solution)/shard_map/reduce_scatter | solution.py:53
  386.8 56.7 %all-to-all-start = ((f32[16,128,512]{2,1,0:T(8,128)}), f32[16,128,512]{2,1,0:T(8,128)}, u32[]{:S(2)}, u32[]{:S(2)}) async-start(f32[16,128,512]{2,1,0:T(8,128)} %stack.2), calls=%async_computation.1 | async-start | bytes 8388608 | tf_op jit(solution)/shard_map/all_to_all | solution.py:63
  391.3 174.4 %all-reduce.8.cloned.1.call-start = ((), (), s32[]{:S(2)}) async-start(), calls=%async_computation.5 | async-start | bytes 4194304 | tf_op jit(solution)/shard_map/psum | solution.py:9
Sparse Core Ops, SparseCore 0:
  12.1 133.3 all-reduce.3
  163.6 112.6 all-reduce.5
  315.8 67.2 reduce-scatter.1
  446.7 118.9 all-reduce.7
